TPU v7x, 256 devices: a whole 4x4x8 slice. The times are simulated.
256 devices in a mesh: row: 8 (over z), col: 32 (over y, x, core).
Axes of the slice: x: 4, y: 4, z: 8, core: 2. Of those that a mesh axis runs over, the one named last changes fastest.
Arguments:
- factor_tiles: bfloat16 [3, 96, 64, 2048], P(None, 'row', None, 'col'), may hold values from -0.3125 to 0.3125
- tile_row: int32 [3, 96, 32], P(None, 'row', 'col'), may hold values from 0 to 63
- tile_col: int32 [3, 96, 32], P(None, 'row', 'col'), may hold values from 0 to 15
- right_sides: float32 [4, 512, 64, 128], P(None, ('col', 'row')), may hold values from -6 to 6
- diag_inverse: float32 [4, 64, 32768], P(None, None, ('col', 'row')), as said below
Outputs:
- preconditioned: float32 [4, 512, 64, 128], P(None, ('col', 'row'))
Inputs may be any that keep to these rules, and one draw needn't show every extreme that they name: `tile_row`: a block row within its row group. `tile_col`: a block column within its column group. `diag_inverse`: diagonal entries of every block between 0.5 and 2.
All inputs are finite; a program needn't handle non-finite values.
Results may differ from a plain program's by a relative error of at most 0.025.
Values may be sent and summed in bfloat16 or wider, within the bound.
A program may use at most 64 MiB of HBM per device.

v0:
```python
import jax
import jax.numpy as jnp
from jax import lax
from jax.sharding import PartitionSpec as P


def apply_inverse(inverse, vector, transposed):
    matrix = inverse.reshape(inverse.shape[0], -1, inverse.shape[0])
    if transposed:
        return jnp.einsum("cir,irn->icn", matrix, vector, precision=lax.Precision.HIGHEST)
    return jnp.einsum("cir,icn->irn", matrix, vector, precision=lax.Precision.HIGHEST)


def solve_all(factor_tiles, tile_row, tile_col, right_sides, diag_inverse):
    levels = factor_tiles.shape[0]
    rows_dev = right_sides.shape[1]
    group_rows = rows_dev * lax.axis_size("row")
    row_ids = tile_row[:, :, 0]
    col_ids = tile_col[:, :, 0]
    current = apply_inverse(diag_inverse[0], right_sides[0], False)
    solved = [current]
    for section_no in range(1, levels + 1):
        gathered = lax.all_gather(current.astype(jnp.bfloat16), "row", axis=0, tiled=True)
        picked = gathered[col_ids[section_no - 1]]
        products = jnp.einsum(
            "tab,tbn->tan", factor_tiles[section_no - 1], picked, preferred_element_type=jnp.float32
        )
        targets = row_ids[section_no - 1]

        def term(offset, length, products=products, targets=targets):
            places = jnp.arange(length, dtype=jnp.int32)
            select = (targets[:, None] == places[None, :]).astype(jnp.float32)
            return jnp.einsum("tq,tan->qan", select, products, precision=lax.Precision.HIGHEST)

        row_sums = lax.psum_scatter(
            term(jnp.int32(0), lax.axis_size("col") * rows_dev).astype(jnp.bfloat16),
            "col",
            scatter_dimension=0,
            tiled=True,
        ).astype(jnp.float32)
        current = apply_inverse(diag_inverse[section_no], right_sides[section_no] - row_sums, False)
        solved.append(current)
    current = apply_inverse(diag_inverse[levels], solved[levels], True)
    result = [current]
    columns_here = jnp.arange(group_rows, dtype=jnp.int32)
    for section_no in range(levels - 1, -1, -1):
        everyone = lax.all_gather(current.astype(jnp.bfloat16), "col", axis=0, tiled=True)
        picked = everyone[row_ids[section_no]]
        spread = jnp.einsum(
            "tab,tan->tbn", factor_tiles[section_no], picked, preferred_element_type=jnp.float32
        )
        select = (col_ids[section_no][:, None] == columns_here[None, :]).astype(jnp.float32)
        column_sums = jnp.einsum("tj,tbn->jbn", select, spread, precision=lax.Precision.HIGHEST)
        received = lax.psum_scatter(
            column_sums.astype(jnp.bfloat16), "row", scatter_dimension=0, tiled=True
        ).astype(jnp.float32)
        current = apply_inverse(diag_inverse[section_no], solved[section_no] - received, True)
        result.insert(0, current)
    return jnp.stack(result)


def on_device(factor_tiles, tile_row, tile_col, right_sides, diag_inverse):
    return solve_all(factor_tiles, tile_row, tile_col, right_sides, diag_inverse)


def solution(mesh):
    return jax.shard_map(
        on_device,
        mesh=mesh,
        in_specs=(
            P(None, "row", None, "col"),
            P(None, "row", "col"),
            P(None, "row", "col"),
            P(None, ("col", "row"), None, None),
            P(None, None, ("col", "row")),
        ),
        out_specs=P(None, ("col", "row"), None, None),
        check_vma=False,
    )
```

profile of v0, /device:TPU:2, one launch (start us, length us, event | category | flops | bytes accessed | tf_op | source)
XLA Modules:
  0.0 630.8 jit_solution(13500943562827002383)
XLA Ops:
  6.5 0.9 fusion.66
  7.4 0.1 copy.45
  7.5 1.0 fusion.67
  8.6 28.6 %all_gather.18 = bf16[16,64,128]{2,1,0:T(8,128)(2,1)S(1)} all-gather(bf16[2,64,128]{2,1,0:T(8,128)(2,1)S(1)} %get-tuple-element.21), channel_id=1, replica_groups=mesh['row'=8,'col'=32] {'row'}, dimensions={0}, use_global_device_ids=true | all-gather | bytes 294912 | tf_op jit(solution)/shard_map/all_gather | solution.py:23
  37.1 0.7 fusion.62
  37.8 0.7 slice_bitcast_fusion
  38.5 0.6 gather_fusion
  39.1 0.2 convolution_bitcast_fusion.2
  39.3 1.1 convolution_convert_fusion.2
  40.4 1.7 copy.47
  42.1 0.0 reduce-scatter.7.cloned.1.call-update
  42.1 0.0 reduce-scatter.9.cloned.1.call-start
  42.2 0.1 copy.48
  42.3 84.0 %reduce-scatter.7.cloned.1.call-done = bf16[2,64,128]{2,1,0:T(8,128)(2,1)} async-done(((bf16[64,64,128]{2,1,0:T(8,128)(2,1)}), bf16[2,64,128]{2,1,0:T(8,128)(2,1)}) %reduce-scatter.7.cloned.1.call-update) | async-done | bytes 32784 | tf_op jit(solution)/shard_map/reduce_scatter | solution.py:35
  126.3 1.0 fusion.68
  127.3 26.2 %all_gather.19 = bf16[16,64,128]{2,1,0:T(8,128)(2,1)S(1)} all-gather(bf16[2,64,128]{2,1,0:T(8,128)(2,1)S(1)} %get-tuple-element.23), channel_id=1, replica_groups=mesh['row'=8,'col'=32] {'row'}, dimensions={0}, use_global_device_ids=true | all-gather | bytes 294912 | tf_op jit(solution)/shard_map/all_gather | solution.py:23
  153.5 0.6 gather_fusion.1
  154.1 0.2 convolution_bitcast_fusion.1
  154.3 1.1 convolution_convert_fusion.1
  155.4 1.7 copy.50
  157.1 0.0 reduce-scatter.9.cloned.1.call-update
  157.1 0.0 reduce-scatter.11.cloned.1.call-start
  157.2 0.1 copy.51
  157.3 83.2 %reduce-scatter.9.cloned.1.call-done = bf16[2,64,128]{2,1,0:T(8,128)(2,1)} async-done(((bf16[64,64,128]{2,1,0:T(8,128)(2,1)}), bf16[2,64,128]{2,1,0:T(8,128)(2,1)}) %reduce-scatter.9.cloned.1.call-update) | async-done | bytes 32784 | tf_op jit(solution)/shard_map/reduce_scatter | solution.py:35
  240.5 1.0 fusion.69
  241.5 26.3 %all_gather.20 = bf16[16,64,128]{2,1,0:T(8,128)(2,1)S(1)} all-gather(bf16[2,64,128]{2,1,0:T(8,128)(2,1)S(1)} %get-tuple-element.25), channel_id=1, replica_groups=mesh['row'=8,'col'=32] {'row'}, dimensions={0}, use_global_device_ids=true | all-gather | bytes 294912 | tf_op jit(solution)/shard_map/all_gather | solution.py:23
  267.8 0.6 gather_fusion.2
  268.4 0.2 convolution_bitcast_fusion
  268.6 1.1 convolution_convert_fusion
  269.7 1.7 copy.53
  271.4 0.0 reduce-scatter.11.cloned.1.call-update
  271.4 0.0 all-gather.4.cloned.1.call-start
  271.4 0.1 reshape_squeeze.19
  271.5 83.2 %reduce-scatter.11.cloned.1.call-done = bf16[2,64,128]{2,1,0:T(8,128)(2,1)} async-done(((bf16[64,64,128]{2,1,0:T(8,128)(2,1)}), bf16[2,64,128]{2,1,0:T(8,128)(2,1)}) %reduce-scatter.11.cloned.1.call-update) | async-done | bytes 32784 | tf_op jit(solution)/shard_map/reduce_scatter | solution.py:35
  354.7 1.0 fusion.21
  355.7 0.8 bitcast_convert_fusion.2
  356.6 0.0 reduce-scatter.13.cloned.1.call-start
  356.7 48.0 %all-gather.4.cloned.1.call-done = bf16[64,64,128]{2,1,0:T(8,128)(2,1)} async-done(((bf16[2,64,128]{2,1,0:T(8,128)(2,1)}), bf16[64,64,128]{2,1,0:T(8,128)(2,1)}) %all-gather.4.cloned.1.call-update) | async-done | bytes 1048592 | tf_op jit(solution)/shard_map/all_gather | solution.py:47
  404.7 1.8 gather_fusion.3
  406.5 0.3 convolution_bitcast_fusion.5
  406.7 0.6 fusion.4
  407.3 0.8 copy.95
  408.1 0.0 reduce-scatter.13.cloned.1.call-update
  408.1 0.0 all-gather.6.cloned.1.call-start
  408.2 36.5 %reduce-scatter.13.cloned.1.call-done = bf16[2,64,128]{2,1,0:T(8,128)(2,1)} async-done(((bf16[16,64,128]{2,1,0:T(8,128)(2,1)}), bf16[2,64,128]{2,1,0:T(8,128)(2,1)}) %reduce-scatter.13.cloned.1.call-update) | async-done | bytes 32784 | tf_op jit(solution)/shard_map/reduce_scatter | solution.py:54
  444.7 1.7 bitcast_convert_fusion.1
  446.4 0.0 reduce-scatter.15.cloned.1.call-start
  446.4 46.9 %all-gather.6.cloned.1.call-done = bf16[64,64,128]{2,1,0:T(8,128)(2,1)} async-done(((bf16[2,64,128]{2,1,0:T(8,128)(2,1)}), bf16[64,64,128]{2,1,0:T(8,128)(2,1)}) %all-gather.6.cloned.1.call-update) | async-done | bytes 1048592 | tf_op jit(solution)/shard_map/all_gather | solution.py:47
  493.3 1.8 gather_fusion.4
  495.1 0.3 convolution_bitcast_fusion.4
  495.4 0.6 fusion.2
  496.0 0.8 copy.94
  496.8 0.0 all-gather.8.cloned.1.call-start
  496.8 36.5 %reduce-scatter.15.cloned.1.call-done = bf16[2,64,128]{2,1,0:T(8,128)(2,1)} async-done(((bf16[16,64,128]{2,1,0:T(8,128)(2,1)}), bf16[2,64,128]{2,1,0:T(8,128)(2,1)}) %reduce-scatter.15.cloned.1.call-update) | async-done | bytes 32784 | tf_op jit(solution)/shard_map/reduce_scatter | solution.py:54
  533.4 1.7 bitcast_convert_fusion
  535.0 0.0 reduce-scatter.17.cloned.1.call-start
  535.1 47.3 %all-gather.8.cloned.1.call-done = bf16[64,64,128]{2,1,0:T(8,128)(2,1)} async-done(((bf16[2,64,128]{2,1,0:T(8,128)(2,1)}), bf16[64,64,128]{2,1,0:T(8,128)(2,1)}) %all-gather.8.cloned.1.call-update) | async-done | bytes 1048592 | tf_op jit(solution)/shard_map/all_gather | solution.py:47
  582.4 1.8 gather_fusion.5
  584.2 0.3 convolution_bitcast_fusion.3
  584.5 0.6 fusion
  585.1 0.8 copy.93
  585.9 36.6 %reduce-scatter.17.cloned.1.call-done = bf16[2,64,128]{2,1,0:T(8,128)(2,1)} async-done(((bf16[16,64,128]{2,1,0:T(8,128)(2,1)}), bf16[2,64,128]{2,1,0:T(8,128)(2,1)}) %reduce-scatter.17.cloned.1.call-update) | async-done | bytes 32784 | tf_op jit(solution)/shard_map/reduce_scatter | solution.py:54
  622.5 1.0 convolution_bitcast_fusion.6
  623.5 0.7 pad_maximum_fusion
  (22 shorter events, 0.1 us)
Async XLA Ops:
  6.5 32.6 %copy-start = (bf16[3,12,64,64]{3,2,1,0:T(8,128)(2,1)S(1)}, bf16[3,12,64,64]{3,2,1,0:T(8,128)(2,1)}, u32[]{:S(2)}) copy-start(bf16[3,12,64,64]{3,2,1,0:T(8,128)(2,1)} %param.5) | copy-start | bytes 884740
  6.5 119.8 %reduce-scatter.7.cloned.1.call-start = ((), (), s32[]{:S(2)}) async-start(), calls=%async_computation.6 | async-start | bytes 1081344 | tf_op jit(solution)/shard_map/reduce_scatter | solution.py:35
  42.1 84.2 %copy-start.1 = (f32[4,2,64,128]{3,2,1,0:T(8,128)S(1)}, f32[4,2,64,128]{3,2,1,0:T(8,128)}, u32[]{:S(2)}) copy-start(f32[4,2,64,128]{3,2,1,0:T(8,128)} %param.8) | copy-start | bytes 786436
  42.1 198.4 %reduce-scatter.9.cloned.1.call-start = ((), (), s32[]{:S(2)}) async-start(), calls=%async_computation.7 | async-start | bytes 1081344 | tf_op jit(solution)/shard_map/reduce_scatter | solution.py:35
  157.1 197.6 %reduce-scatter.11.cloned.1.call-start = ((), (), s32[]{:S(2)}) async-start(), calls=%async_computation.8 | async-start | bytes 1081344 | tf_op jit(solution)/shard_map/reduce_scatter | solution.py:35
  271.4 85.3 %copy-start.2 = (s32[3,12,1]{1,2,0:T(1,128)S(1)}, s32[3,12,1]{1,2,0:T(1,128)}, u32[]{:S(2)}) copy-start(s32[3,12,1]{1,2,0:T(1,128)} %param.6) | copy-start | bytes 436
  271.4 85.3 %copy-start.3 = (s32[3,12,1]{1,2,0:T(1,128)S(1)}, s32[3,12,1]{1,2,0:T(1,128)}, u32[]{:S(2)}) copy-start(s32[3,12,1]{1,2,0:T(1,128)} %param.7) | copy-start | bytes 436
  271.4 133.3 %all-gather.4.cloned.1.call-start = ((), (), s32[]{:S(2)}) async-start(), calls=%async_computation.9 | async-start | bytes 1081344 | tf_op jit(solution)/shard_map/all_gather | solution.py:47
  356.6 88.1 %reduce-scatter.13.cloned.1.call-start = ((), (), s32[]{:S(2)}) async-start(), calls=%async_computation.10 | async-start | bytes 294912 | tf_op jit(solution)/shard_map/reduce_scatter | solution.py:54
  408.1 85.2 %all-gather.6.cloned.1.call-start = ((), (), s32[]{:S(2)}) async-start(), calls=%async_computation.11 | async-start | bytes 1081344 | tf_op jit(solution)/shard_map/all_gather | solution.py:47
  446.4 87.0 %reduce-scatter.15.cloned.1.call-start = ((), (), s32[]{:S(2)}) async-start(), calls=%async_computation.12 | async-start | bytes 294912 | tf_op jit(solution)/shard_map/reduce_scatter | solution.py:54
  496.8 85.7 %all-gather.8.cloned.1.call-start = ((), (), s32[]{:S(2)}) async-start(), calls=%async_computation.13 | async-start | bytes 1081344 | tf_op jit(solution)/shard_map/all_gather | solution.py:47
  535.0 87.4 %reduce-scatter.17.cloned.1.call-start = ((), (), s32[]{:S(2)}) async-start(), calls=%async_computation.14 | async-start | bytes 294912 | tf_op jit(solution)/shard_map/reduce_scatter | solution.py:54
Sparse Core Ops, SparseCore 0:
  42.2 84.0 reduce-scatter.6
  157.2 83.2 reduce-scatter.8
  271.5 83.1 reduce-scatter.10
  357.4 47.1 all-gather.3
  408.2 36.3 reduce-scatter.12
  447.1 46.1 all-gather.5
  496.9 36.4 reduce-scatter.14
  536.2 46.1 all-gather.7
  586.0 36.3 reduce-scatter.16
where the time goes:
time: 631 us
  waiting for transfers between devices  502 us (80%)
  blocking collectives  81.1 us (13%)
  local copies, waits for them, and re-layouts  16.5 us (3%)
  matrix products  15.6 us (2%)
  between operations  13.5 us (2%)
    reduce_scatter x3, waiting for transfers between devices, solve_all(): lax.psum_scatter(term(jnp.int32(0), lax.axis_size('col') * rows_dev).asty...  250 us
    all_gather x3, waiting for transfers between devices, solve_all(): lax.all_gather(current.astype(jnp.bfloat16), 'col', axis=0, tiled=True)  142 us
    reduce_scatter x3, waiting for transfers between devices, solve_all(): lax.psum_scatter(column_sums.astype(jnp.bfloat16), 'row', scatter_dimensi...  110 us
    all_gather x3, blocking collectives, solve_all(): lax.all_gather(current.astype(jnp.bfloat16), 'row', axis=0, tiled=True)  81.1 us
  transfers between devices with their start and end apart: 9, of which 9 were waited for; matrix products, arithmetic and copies ran while one was open for 0% of the time, Pallas kernels for 0%

commit v1 on v0

--- a/solution.py
+++ b/solution.py
@@ -1,7 +1,16 @@
+import functools
 import jax
 import jax.numpy as jnp
 from jax import lax
 from jax.sharding import PartitionSpec as P
+
+
+def put_the_desk(obj, at_axis):
+    q_next = jnp.concatenate([obj for _ in range(lax.axis_size("col"))], axis=at_axis)
+    return lax.all_to_all(q_next, "col", at_axis, at_axis, tiled=True)
+
+
+take_the_column = functools.partial(put_the_desk, at_axis=0)
 
 
 def apply_inverse(inverse, vector, transposed):
@@ -44,7 +53,7 @@
     result = [current]
     columns_here = jnp.arange(group_rows, dtype=jnp.int32)
     for section_no in range(levels - 1, -1, -1):
-        everyone = lax.all_gather(current.astype(jnp.bfloat16), "col", axis=0, tiled=True)
+        everyone = take_the_column(current.astype(jnp.bfloat16))
         picked = everyone[row_ids[section_no]]
         spread = jnp.einsum(
             "tab,tan->tbn", factor_tiles[section_no], picked, preferred_element_type=jnp.float32

time: 631 us -> 603 us (0.956)
  waiting for transfers between devices: 502 us -> 400 us
  local copies, waits for them, and re-layouts: 16.5 us -> 69 us
  starting transfers between devices: 0.34 us -> 21 us
    all_gather x3 -> x0, waiting for transfers between devices: 142 us -> none  [solve_all(): lax.all_gather(current.astype(jnp.bfloat16), 'col', axis=0, tiled=True)]
    unnamed x8 -> x98, local copies, waits for them, and re-layouts: 0.01 us -> 54.4 us
    all_to_all x0 -> x3, waiting for transfers between devices: none -> 48.1 us  [put_the_desk(): return lax.all_to_all(q_next, 'col', at_axis, at_axis, tiled=True)]
    all_to_all x0 -> x3, starting transfers between devices: none -> 20.8 us  [put_the_desk(): return lax.all_to_all(q_next, 'col', at_axis, at_axis, tiled=True)]
    reduce_scatter x3, waiting for transfers between devices: 110 us -> 101 us  [solve_all(): lax.psum_scatter(column_sums.astype(jnp.bfloat16), 'row', scatter_dimensi...]
where the time goes in v1:
time: 603 us; the launch traced here: 602 us
  waiting for transfers between devices  400 us (66%)
  blocking collectives  81.1 us (13%)
  local copies, waits for them, and re-layouts  69 us (11%)
  starting transfers between devices  21 us (3%)
  matrix products  15.6 us (3%)
  between operations  13.8 us (2%)
    reduce_scatter x3, waiting for transfers between devices, solve_all(): lax.psum_scatter(term(jnp.int32(0), lax.axis_size('col') * rows_dev).asty...  250 us
    reduce_scatter x3, waiting for transfers between devices, solve_all(): lax.psum_scatter(column_sums.astype(jnp.bfloat16), 'row', scatter_dimensi...  101 us
    all_gather x3, blocking collectives, solve_all(): lax.all_gather(current.astype(jnp.bfloat16), 'row', axis=0, tiled=True)  81.1 us
    unnamed x98, local copies, waits for them, and re-layouts  54.4 us
    all_to_all x3, waiting for transfers between devices, put_the_desk(): return lax.all_to_all(q_next, 'col', at_axis, at_axis, tiled=True)  48.1 us
    all_to_all x3, starting transfers between devices, put_the_desk(): return lax.all_to_all(q_next, 'col', at_axis, at_axis, tiled=True)  20.8 us
  transfers between devices with their start and end apart: 9, of which 9 were waited for; matrix products, arithmetic and copies ran while one was open for 0% of the time, Pallas kernels for 0%

profile of v1, /device:TPU:2, one launch (start us, length us, event | category | flops | bytes accessed | tf_op | source)
XLA Modules:
  0.0 602.2 jit_solution(17335023149326834566)
XLA Ops:
  6.5 0.9 fusion.66
  7.5 1.0 fusion.67
  8.6 28.6 %all_gather.9 = bf16[16,64,128]{2,1,0:T(8,128)(2,1)S(1)} all-gather(bf16[2,64,128]{2,1,0:T(8,128)(2,1)S(1)} %get-tuple-element.27), channel_id=1, replica_groups=mesh['row'=8,'col'=32] {'row'}, dimensions={0}, use_global_device_ids=true | all-gather | bytes 294912 | tf_op jit(solution)/shard_map/all_gather | solution.py:32
  37.1 0.7 fusion.62
  37.8 0.7 slice_bitcast_fusion
  39.3 1.1 convolution_convert_fusion.2
  40.4 1.7 copy.47
  42.3 84.0 %reduce-scatter.7.cloned.1.call-done = bf16[2,64,128]{2,1,0:T(8,128)(2,1)} async-done(((bf16[64,64,128]{2,1,0:T(8,128)(2,1)}), bf16[2,64,128]{2,1,0:T(8,128)(2,1)}) %reduce-scatter.7.cloned.1.call-update) | async-done | bytes 32784 | tf_op jit(solution)/shard_map/reduce_scatter | solution.py:44
  126.3 1.0 fusion.68
  127.3 26.2 %all_gather.10 = bf16[16,64,128]{2,1,0:T(8,128)(2,1)S(1)} all-gather(bf16[2,64,128]{2,1,0:T(8,128)(2,1)S(1)} %get-tuple-element.29), channel_id=1, replica_groups=mesh['row'=8,'col'=32] {'row'}, dimensions={0}, use_global_device_ids=true | all-gather | bytes 294912 | tf_op jit(solution)/shard_map/all_gather | solution.py:32
  154.3 1.1 convolution_convert_fusion.1
  155.4 1.7 copy.50
  157.3 83.2 %reduce-scatter.9.cloned.1.call-done = bf16[2,64,128]{2,1,0:T(8,128)(2,1)} async-done(((bf16[64,64,128]{2,1,0:T(8,128)(2,1)}), bf16[2,64,128]{2,1,0:T(8,128)(2,1)}) %reduce-scatter.9.cloned.1.call-update) | async-done | bytes 32784 | tf_op jit(solution)/shard_map/reduce_scatter | solution.py:44
  240.5 1.0 fusion.69
  241.5 26.3 %all_gather.11 = bf16[16,64,128]{2,1,0:T(8,128)(2,1)S(1)} all-gather(bf16[2,64,128]{2,1,0:T(8,128)(2,1)S(1)} %get-tuple-element.31), channel_id=1, replica_groups=mesh['row'=8,'col'=32] {'row'}, dimensions={0}, use_global_device_ids=true | all-gather | bytes 294912 | tf_op jit(solution)/shard_map/all_gather | solution.py:32
  268.6 1.1 convolution_convert_fusion
  269.7 1.7 copy.53
  271.5 83.2 %reduce-scatter.11.cloned.1.call-done = bf16[2,64,128]{2,1,0:T(8,128)(2,1)} async-done(((bf16[64,64,128]{2,1,0:T(8,128)(2,1)}), bf16[2,64,128]{2,1,0:T(8,128)(2,1)}) %reduce-scatter.11.cloned.1.call-update) | async-done | bytes 32784 | tf_op jit(solution)/shard_map/reduce_scatter | solution.py:44
  354.7 1.0 fusion.21
  355.8 0.8 constant_dynamic-update-slice_fusion.31
  359.6 0.6 constant_dynamic-update-slice_fusion.25
  360.8 0.6 constant_dynamic-update-slice_fusion.23
  362.0 0.6 constant_dynamic-update-slice_fusion.21
  367.4 0.6 constant_dynamic-update-slice_fusion.12
  368.1 0.6 constant_dynamic-update-slice_fusion.11
  369.3 0.6 constant_dynamic-update-slice_fusion.9
  369.9 0.6 constant_dynamic-update-slice_fusion.8
  370.5 0.6 constant_dynamic-update-slice_fusion.7
  371.7 0.6 constant_dynamic-update-slice_fusion.5
  372.9 0.6 constant_dynamic-update-slice_fusion.3
  375.3 6.0 all-to-all-start
  381.4 16.0 %all-to-all-done = bf16[64,64,128]{2,1,0:T(8,128)(2,1)S(1)} async-done(((bf16[64,64,128]{2,1,0:T(8,128)(2,1)}), bf16[64,64,128]{2,1,0:T(8,128)(2,1)S(1)}, u32[]{:S(2)}, u32[]{:S(2)}) %all-to-all-start) | async-done | bytes 1048608 | tf_op jit(solution)/shard_map/all_to_all | solution.py:10
  398.9 0.8 copy.95
  399.7 35.6 %reduce-scatter.13.cloned.1.call-done = bf16[2,64,128]{2,1,0:T(8,128)(2,1)} async-done(((bf16[16,64,128]{2,1,0:T(8,128)(2,1)}), bf16[2,64,128]{2,1,0:T(8,128)(2,1)}) %reduce-scatter.13.cloned.1.call-update) | async-done | bytes 32784 | tf_op jit(solution)/shard_map/reduce_scatter | solution.py:63
  435.2 1.7 constant_dynamic-update-slice_fusion.63
  439.9 0.6 constant_dynamic-update-slice_fusion.57
  441.1 0.6 constant_dynamic-update-slice_fusion.55
  442.3 0.6 constant_dynamic-update-slice_fusion.53
  447.8 0.6 constant_dynamic-update-slice_fusion.44
  449.6 0.6 constant_dynamic-update-slice_fusion.41
  450.2 0.6 constant_dynamic-update-slice_fusion.40
  450.8 0.6 constant_dynamic-update-slice_fusion.39
  452.0 0.6 constant_dynamic-update-slice_fusion.37
  453.2 0.6 constant_dynamic-update-slice_fusion.35
  455.7 7.4 %all-to-all-start.1 = ((bf16[64,64,128]{2,1,0:T(8,128)(2,1)}), bf16[64,64,128]{2,1,0:T(8,128)(2,1)S(1)}, u32[]{:S(2)}, u32[]{:S(2)}) async-start(bf16[64,64,128]{2,1,0:T(8,128)(2,1)} %constant_dynamic-update-slice_fusion.32), calls=%async_computation.5 | async-start | bytes 2097152 | tf_op jit(solution)/shard_map/all_to_all | solution.py:10
  463.1 16.1 %all-to-all-done.1 = bf16[64,64,128]{2,1,0:T(8,128)(2,1)S(1)} async-done(((bf16[64,64,128]{2,1,0:T(8,128)(2,1)}), bf16[64,64,128]{2,1,0:T(8,128)(2,1)S(1)}, u32[]{:S(2)}, u32[]{:S(2)}) %all-to-all-start.1) | async-done | bytes 1048608 | tf_op jit(solution)/shard_map/all_to_all | solution.py:10
  480.6 0.8 copy.94
  481.4 32.9 %reduce-scatter.15.cloned.1.call-done = bf16[2,64,128]{2,1,0:T(8,128)(2,1)} async-done(((bf16[16,64,128]{2,1,0:T(8,128)(2,1)}), bf16[2,64,128]{2,1,0:T(8,128)(2,1)}) %reduce-scatter.15.cloned.1.call-update) | async-done | bytes 32784 | tf_op jit(solution)/shard_map/reduce_scatter | solution.py:63
  514.4 1.7 constant_dynamic-update-slice_fusion.95
  519.1 0.6 constant_dynamic-update-slice_fusion.89
  520.3 0.6 constant_dynamic-update-slice_fusion.87
  521.5 0.6 constant_dynamic-update-slice_fusion.85
  526.9 0.6 constant_dynamic-update-slice_fusion.76
  528.7 0.6 constant_dynamic-update-slice_fusion.73
  529.4 0.6 constant_dynamic-update-slice_fusion.72
  530.0 0.6 constant_dynamic-update-slice_fusion.71
  531.2 0.6 constant_dynamic-update-slice_fusion.69
  532.4 0.6 constant_dynamic-update-slice_fusion.67
  534.8 7.4 %all-to-all-start.2 = ((bf16[64,64,128]{2,1,0:T(8,128)(2,1)}), bf16[64,64,128]{2,1,0:T(8,128)(2,1)S(1)}, u32[]{:S(2)}, u32[]{:S(2)}) async-start(bf16[64,64,128]{2,1,0:T(8,128)(2,1)} %constant_dynamic-update-slice_fusion.64), calls=%async_computation.7 | async-start | bytes 2097152 | tf_op jit(solution)/shard_map/all_to_all | solution.py:10
  542.3 16.1 %all-to-all-done.2 = bf16[64,64,128]{2,1,0:T(8,128)(2,1)S(1)} async-done(((bf16[64,64,128]{2,1,0:T(8,128)(2,1)}), bf16[64,64,128]{2,1,0:T(8,128)(2,1)S(1)}, u32[]{:S(2)}, u32[]{:S(2)}) %all-to-all-start.2) | async-done | bytes 1048608 | tf_op jit(solution)/shard_map/all_to_all | solution.py:10
  559.8 0.8 copy.93
  560.6 33.0 %reduce-scatter.17.cloned.1.call-done = bf16[2,64,128]{2,1,0:T(8,128)(2,1)} async-done(((bf16[16,64,128]{2,1,0:T(8,128)(2,1)}), bf16[2,64,128]{2,1,0:T(8,128)(2,1)}) %reduce-scatter.17.cloned.1.call-update) | async-done | bytes 32784 | tf_op jit(solution)/shard_map/reduce_scatter | solution.py:63
  593.5 1.0 convolution_bitcast_fusion.6
  594.6 0.7 pad_maximum_fusion
  (112 shorter events, 46.5 us)
Async XLA Ops:
  6.5 32.6 %copy-start = (bf16[3,12,64,64]{3,2,1,0:T(8,128)(2,1)S(1)}, bf16[3,12,64,64]{3,2,1,0:T(8,128)(2,1)}, u32[]{:S(2)}) copy-start(bf16[3,12,64,64]{3,2,1,0:T(8,128)(2,1)} %param.5) | copy-start | bytes 884740
  6.5 119.8 %reduce-scatter.7.cloned.1.call-start = ((), (), s32[]{:S(2)}) async-start(), calls=%async_computation.9 | async-start | bytes 1081344 | tf_op jit(solution)/shard_map/reduce_scatter | solution.py:44
  42.1 84.2 %copy-start.1 = (f32[4,2,64,128]{3,2,1,0:T(8,128)S(1)}, f32[4,2,64,128]{3,2,1,0:T(8,128)}, u32[]{:S(2)}) copy-start(f32[4,2,64,128]{3,2,1,0:T(8,128)} %param.8) | copy-start | bytes 786436
  42.1 198.4 %reduce-scatter.9.cloned.1.call-start = ((), (), s32[]{:S(2)}) async-start(), calls=%async_computation.10 | async-start | bytes 1081344 | tf_op jit(solution)/shard_map/reduce_scatter | solution.py:44
  157.1 197.6 %reduce-scatter.11.cloned.1.call-start = ((), (), s32[]{:S(2)}) async-start(), calls=%async_computation.11 | async-start | bytes 1081344 | tf_op jit(solution)/shard_map/reduce_scatter | solution.py:44
  375.3 6.0 %copy-start.2 = (s32[3,12,1]{1,2,0:T(1,128)S(1)}, s32[3,12,1]{1,2,0:T(1,128)}, u32[]{:S(2)}) copy-start(s32[3,12,1]{1,2,0:T(1,128)} %param.6) | copy-start | bytes 436
  375.3 6.1 %copy-start.3 = (s32[3,12,1]{1,2,0:T(1,128)S(1)}, s32[3,12,1]{1,2,0:T(1,128)}, u32[]{:S(2)}) copy-start(s32[3,12,1]{1,2,0:T(1,128)} %param.7) | copy-start | bytes 436
  375.3 22.1 %all-to-all-start = ((bf16[64,64,128]{2,1,0:T(8,128)(2,1)}), bf16[64,64,128]{2,1,0:T(8,128)(2,1)S(1)}, u32[]{:S(2)}, u32[]{:S(2)}) async-start(bf16[64,64,128]{2,1,0:T(8,128)(2,1)} %constant_dynamic-update-slice_fusion), calls=%async_computation.3 | async-start | bytes 2097152 | tf_op jit(solution)/shard_map/all_to_all | solution.py:10
  381.3 53.9 %reduce-scatter.13.cloned.1.call-start = ((), (), s32[]{:S(2)}) async-start(), calls=%async_computation.12 | async-start | bytes 294912 | tf_op jit(solution)/shard_map/reduce_scatter | solution.py:63
  455.7 23.5 %all-to-all-start.1 = ((bf16[64,64,128]{2,1,0:T(8,128)(2,1)}), bf16[64,64,128]{2,1,0:T(8,128)(2,1)S(1)}, u32[]{:S(2)}, u32[]{:S(2)}) async-start(bf16[64,64,128]{2,1,0:T(8,128)(2,1)} %constant_dynamic-update-slice_fusion.32), calls=%async_computation.5 | async-start | bytes 2097152 | tf_op jit(solution)/shard_map/all_to_all | solution.py:10
  463.1 51.3 %reduce-scatter.15.cloned.1.call-start = ((), (), s32[]{:S(2)}) async-start(), calls=%async_computation.13 | async-start | bytes 294912 | tf_op jit(solution)/shard_map/reduce_scatter | solution.py:63
  534.8 23.5 %all-to-all-start.2 = ((bf16[64,64,128]{2,1,0:T(8,128)(2,1)}), bf16[64,64,128]{2,1,0:T(8,128)(2,1)S(1)}, u32[]{:S(2)}, u32[]{:S(2)}) async-start(bf16[64,64,128]{2,1,0:T(8,128)(2,1)} %constant_dynamic-update-slice_fusion.64), calls=%async_computation.7 | async-start | bytes 2097152 | tf_op jit(solution)/shard_map/all_to_all | solution.py:10
  542.2 51.3 %reduce-scatter.17.cloned.1.call-start = ((), (), s32[]{:S(2)}) async-start(), calls=%async_computation.14 | async-start | bytes 294912 | tf_op jit(solution)/shard_map/reduce_scatter | solution.py:63
Sparse Core Ops, SparseCore 0:
  42.2 84.0 reduce-scatter.6
  157.2 83.2 reduce-scatter.8
  271.5 83.1 reduce-scatter.10
  399.8 35.3 reduce-scatter.12
  481.6 32.7 reduce-scatter.14
  560.7 32.7 reduce-scatter.16
